TPU v7x, 32 devices: a whole 2x2x4 slice. The times are simulated.
32 devices in a mesh: groups: 2 (over y), space: 4 (over z), tm: 2 (over x), chan: 2 (over core).
Axes of the slice: x: 2, y: 2, z: 4, core: 2. Of those that a mesh axis runs over, the one named last changes fastest.
Arguments:
- hidden_states: bfloat16 [8, 4, 64, 512], P(('groups', 'tm'), 'space', None, 'chan'), parts along dimension 0, may hold values from -25 to 25
- first_gain: float32 [512], P('chan'), may hold values from 0.1 to 1.9
- second_gain: float32 [512], P('chan'), may hold values from 0.1 to 1.9
- query_weight: bfloat16 [512, 512], replicated, may hold values from -0.4861359 to 0.4861359
- key_weight: bfloat16 [512, 512], replicated, may hold values from -0.4861359 to 0.4861359
- value_weight: bfloat16 [512, 512], replicated, may hold values from -0.25 to 0.25
- out_weight: bfloat16 [512, 512], replicated, may hold values from -0.25 to 0.25
- conv_kernel: bfloat16 [3, 3, 3, 512, 512], P(None, None, None, 'tm', 'chan'), may hold values from -0.0546875 to 0.0546875
Outputs:
- attended: bfloat16 [8, 4, 64, 512], P(('groups', 'tm'), 'space', None, 'chan'), parts along dimension 0
- convolved: bfloat16 [8, 4, 64, 512], P(('groups', 'tm'), 'space', None, 'chan'), parts along dimension 0
There are 2 independent parts, one for each index of `groups`. A program takes and returns all parts, laid end to end along the dimension named above; an argument that names none is the same for every part. Nothing has to cross between parts.
All inputs are finite; a program needn't handle non-finite values.
Results may differ from a plain program's by a relative error of at most 0.012.
The roundings to bfloat16 on the way count: a program that leaves them out, or rounds other values in their place, can miss the bound.
Values may be sent and summed in bfloat16 or wider, within the bound.
A program may use at most 64 MiB of HBM per device.

v0:
```python
import jax
import jax.numpy as jnp
from jax import lax
from jax.sharding import PartitionSpec as P

D = 512
NGROUP = 32
EPSILON = 1e-06


def shifted_2(x, axis, by):
    peers = lax.axis_size(axis)
    pairs = [(i, i + by) for i in range(peers) if 0 <= i + by < peers]
    return lax.ppermute(x, axis, pairs)


def padded_2(cells, sides, width):
    for axis, dim in sides:
        count = lax.axis_size(axis)
        ends = count - 1
        head = lax.slice_in_dim(cells, 0, width, axis=dim)
        tail = lax.slice_in_dim(cells, cells.shape[dim] - width, cells.shape[dim], axis=dim)
        cells = jnp.concatenate(
            [
                lax.ppermute(tail, axis, [(i, (i + 1) % count) for i in range(ends)]),
                cells,
                lax.ppermute(head, axis, [((i + 1) % count, i) for i in range(ends)]),
            ],
            axis=dim,
        )
    return cells


def normalize(source, gain_vector):
    channels = source.shape[3]
    group_width = D // NGROUP
    grouped = source.reshape(-1, channels // group_width, group_width)
    population = grouped.shape[0] * group_width * lax.axis_size("space") * lax.axis_size("tm")
    group_sums, group_squares = lax.psum(
        (jnp.sum(grouped, axis=(0, 2)), jnp.sum(grouped * grouped, axis=(0, 2))), ("space", "tm")
    )
    centre = group_sums / population
    spread = jnp.maximum(group_squares / population - centre * centre, 0.0)
    shifted = grouped - centre[None, :, None]
    scaled = shifted * lax.rsqrt(spread + EPSILON)[None, :, None]
    return scaled.reshape(source.shape) * gain_vector


def attend(normed, query_weight, key_weight, value_weight, out_weight):
    frame_count, row_count, col_count, channels = normed.shape
    token_count = frame_count * row_count * col_count
    tokens = normed.reshape(token_count, channels)
    halves = lax.all_to_all(tokens, "chan", split_axis=0, concat_axis=1, tiled=True)
    half_rows = halves.shape[0]
    queries = jnp.dot(halves, query_weight, preferred_element_type=jnp.float32).astype(jnp.bfloat16)
    keyed = jnp.dot(halves, key_weight, preferred_element_type=jnp.float32).astype(jnp.bfloat16)
    valued = jnp.dot(halves, value_weight, preferred_element_type=jnp.float32).astype(jnp.bfloat16)
    score_scale = D ** (-0.5)
    running_max = jnp.full((half_rows,), -1e30, jnp.float32)
    key_piece = lax.all_gather(keyed, "space", axis=0, tiled=True)
    value_piece = lax.all_gather(valued, "space", axis=0, tiled=True)
    scores = jnp.dot(queries, key_piece.T, preferred_element_type=jnp.float32) * score_scale
    newest_max = jnp.maximum(running_max, jnp.max(scores, axis=1))
    weights = jnp.exp(scores - newest_max[:, None])
    running_sum = jnp.sum(weights, axis=1)
    accumulated = jnp.dot(
        weights.astype(jnp.bfloat16), value_piece, preferred_element_type=jnp.float32
    )
    mixed = (accumulated / running_sum[:, None]).astype(jnp.bfloat16)
    projected = jnp.dot(mixed, out_weight, preferred_element_type=jnp.float32).astype(jnp.bfloat16)
    returned = lax.all_to_all(projected, "chan", split_axis=1, concat_axis=0, tiled=True)
    return returned.reshape(frame_count, row_count, col_count, channels)


def join_channels(activated):
    return lax.all_gather(activated, "chan", axis=3, tiled=True)


def extend(frames_in):
    earlier = shifted_2(frames_in, "tm", 1)
    timed = jnp.concatenate([earlier, frames_in], axis=0)
    rimmed = padded_2(timed, (("space", 1),), 1)
    return jnp.pad(rimmed, ((0, 0), (0, 0), (1, 1), (0, 0)))


def convolve(activated, conv_kernel):
    frame_count, row_count, col_count = (activated.shape[0], activated.shape[1], activated.shape[2])
    padded = extend(join_channels(activated))
    out_width = conv_kernel.shape[4]
    initial = jnp.zeros((frame_count * row_count * col_count, out_width), jnp.float32)
    running_total = initial
    piece = lax.all_gather(conv_kernel, "tm", axis=3, tiled=True)
    for time_tap in range(3):
        for row_tap in range(3):
            for col_tap in range(3):
                window = padded[
                    time_tap : time_tap + frame_count,
                    row_tap : row_tap + row_count,
                    col_tap : col_tap + col_count,
                ]
                window = window.reshape(frame_count * row_count * col_count, piece.shape[3])
                running_total = running_total + jnp.dot(
                    window, piece[time_tap, row_tap, col_tap], preferred_element_type=jnp.float32
                )
    return running_total.reshape(frame_count, row_count, col_count, out_width).astype(jnp.bfloat16)


def on_device(
    hidden_states,
    first_gain,
    second_gain,
    query_weight,
    key_weight,
    value_weight,
    out_weight,
    conv_kernel,
):
    source = hidden_states.astype(jnp.float32)
    normed = normalize(source, first_gain).astype(jnp.bfloat16)
    attended = attend(normed, query_weight, key_weight, value_weight, out_weight)
    resid = source + attended.astype(jnp.float32)
    activated = jax.nn.silu(normalize(resid, second_gain)).astype(jnp.bfloat16)
    convolved = convolve(activated, conv_kernel)
    return (attended, convolved)


def solution(mesh):
    placed = (
        P(("groups", "tm"), "space", None, "chan"),
        P("chan"),
        P("chan"),
        P(),
        P(),
        P(),
        P(),
        P(None, None, None, "tm", "chan"),
    )
    return jax.shard_map(
        on_device,
        mesh=mesh,
        in_specs=placed,
        out_specs=(
            P(("groups", "tm"), "space", None, "chan"),
            P(("groups", "tm"), "space", None, "chan"),
        ),
        check_vma=False,
    )
```

profile of v0, /device:TPU:0, one launch (start us, length us, event | category | flops | bytes accessed | tf_op | source)
XLA Modules:
  0.0 143.7 jit_solution(14035605134556565551)
XLA Ops:
  7.2 0.7 all-gather.2.cloned.1.call-update
  7.9 0.9 convert_reduce_fusion
  8.8 0.1 reduce_sum.58
  8.9 0.1 reduce_sum.61
  9.0 0.1 reduce_sum.59
  9.1 0.1 reduce_sum.62
  9.2 23.3 %all-reduce.2 = (f32[16]{0:T(128)S(1)}, f32[16]{0:T(128)S(1)}) all-reduce(f32[16]{0:T(128)S(1)} %reduce_sum.62, f32[16]{0:T(128)S(1)} %reduce_sum.59), channel_id=1, replica_groups=mesh['groups'=2,'space'=4,'tm'=2,'chan'=2] {'space','tm'}, use_global_device_ids=true, to_apply=%region_5.0 | all-reduce | flops 32 | bytes 256 | tf_op jit(solution)/shard_map/psum | solution.py:39
  32.6 0.1 mul.77
  32.8 0.1 sub.43
  32.9 0.9 fusion.26
  33.7 3.8 %all_to_all.35 = bf16[2,64,256]{2,1,0:T(8,128)(2,1)S(1)} all-to-all(bf16[2,64,256]{2,1,0:T(8,128)(2,1)S(1)} %fusion.26), channel_id=1, replica_groups=mesh['groups'=2,'space'=4,'tm'=2,'chan'=2] {'chan'}, dimensions={0} | all-to-all | bytes 131072 | tf_op jit(solution)/shard_map/all_to_all | solution.py:53
  37.5 0.2 convolution_convert_fusion.2
  37.8 14.3 %all_gather.12 = bf16[256,512]{1,0:T(8,128)(2,1)S(1)} all-gather(bf16[64,512]{1,0:T(8,128)(2,1)S(1)} %convolution_convert_fusion.2), channel_id=1, replica_groups=mesh['groups'=2,'space'=4,'tm'=2,'chan'=2] {'space'}, dimensions={0}, use_global_device_ids=true | all-gather | bytes 327680 | tf_op jit(solution)/shard_map/all_gather | solution.py:60
  52.1 1.2 convolution_convert_fusion.1
  53.3 13.9 %all_gather.13 = bf16[256,512]{1,0:T(8,128)(2,1)S(1)} all-gather(bf16[64,512]{1,0:T(8,128)(2,1)S(1)} %convolution_convert_fusion.1), channel_id=1, replica_groups=mesh['groups'=2,'space'=4,'tm'=2,'chan'=2] {'space'}, dimensions={0}, use_global_device_ids=true | all-gather | bytes 327680 | tf_op jit(solution)/shard_map/all_gather | solution.py:61
  67.2 1.5 %fusion.37 = (f32[64]{0:T(128)S(1)}, f32[64,256]{1,0:T(8,128)S(1)}) fusion(bf16[256,512]{1,0:T(8,128)(2,1)S(1)} %all_gather.12, bf16[64,512]{1,0:T(8,128)(2,1)S(1)} %bitcast.164, bf16[512,512]{1,0:T(8,128)(2,1)} %param.11), kind=kOutput, calls=%fused_computation.104 | convolution fusion | flops 50397120 | bytes 917760 | tf_op jit(solution)/shard_map/dot_general | solution.py:62
  68.7 0.2 fusion.28
  68.9 1.4 convolution_convert_fusion
  70.3 3.8 %all_to_all.36 = bf16[64,2,256]{2,0,1:T(8,128)(2,1)S(1)} all-to-all(bf16[64,2,256]{2,0,1:T(8,128)(2,1)S(1)} %bitcast.193), channel_id=1, replica_groups=mesh['groups'=2,'space'=4,'tm'=2,'chan'=2] {'chan'}, dimensions={1} | all-to-all | bytes 131072 | tf_op jit(solution)/shard_map/all_to_all | solution.py:71
  74.2 0.1 reduce_sum.81
  74.3 0.1 reduce_sum.82
  74.5 0.1 reduce_sum.85
  74.6 17.4 %all-reduce.1 = (f32[16]{0:T(128)S(1)}, f32[16]{0:T(128)S(1)}) all-reduce(f32[16]{0:T(128)S(1)} %reduce_sum.85, f32[16]{0:T(128)S(1)} %reduce_sum.82), channel_id=1, replica_groups=mesh['groups'=2,'space'=4,'tm'=2,'chan'=2] {'space','tm'}, use_global_device_ids=true, to_apply=%region_13.14 | all-reduce | flops 32 | bytes 256 | tf_op jit(solution)/shard_map/psum | solution.py:39
  92.1 0.1 mul.87
  92.3 0.1 sub.50
  92.4 1.9 %all_gather.14 = bf16[2,1,64,512]{3,2,1,0:T(8,128)(2,1)S(1)} all-gather(bf16[2,1,64,256]{3,2,1,0:T(8,128)(2,1)S(1)} %multiply_convert_fusion), channel_id=1, replica_groups=mesh['groups'=2,'space'=4,'tm'=2,'chan'=2] {'chan'}, dimensions={3}, use_global_device_ids=true | all-gather | bytes 196608 | tf_op jit(solution)/shard_map/all_gather | solution.py:76
  94.3 4.1 %collective-permute-start = (bf16[2,1,64,512]{3,2,1,0:T(8,128)(2,1)S(1)}, bf16[2,1,64,512]{3,2,1,0:T(8,128)(2,1)S(1)}, u32[]{:S(2)}, u32[]{:S(2)}) collective-permute-start(bf16[2,1,64,512]{3,2,1,0:T(8,128)(2,1)S(1)} %all_gather.14), channel_id=1, source_target_pairs={{0,2},{1,3},{4,6},{5,7},{8,10},{9,11},{12,14},{13,15},{16,18},{17,... | collective-permute-start | bytes 393224 | tf_op jit(solution)/shard_map/ppermute | solution.py:14
  98.4 4.3 %collective-permute-done = bf16[2,1,64,512]{3,2,1,0:T(8,128)(2,1)S(1)} collective-permute-done((bf16[2,1,64,512]{3,2,1,0:T(8,128)(2,1)S(1)}, bf16[2,1,64,512]{3,2,1,0:T(8,128)(2,1)S(1)}, u32[]{:S(2)}, u32[]{:S(2)}) %collective-permute-start) | collective-permute-done | bytes 131104 | tf_op jit(solution)/shard_map/ppermute | solution.py:14
  102.8 3.0 %collective-permute-start.1 = (bf16[4,1,64,512]{3,2,1,0:T(8,128)(2,1)S(1)}, bf16[4,1,64,512]{3,2,1,0:T(8,128)(2,1)S(1)}, u32[]{:S(2)}, u32[]{:S(2)}) collective-permute-start(bf16[4,1,64,512]{3,2,1,0:T(8,128)(2,1)S(1)} %constant_dynamic-update-slice_fusion), channel_id=1, source_target_pairs={{0,4},{4,8},{8,12},{1,5},{5,9},{9,13},{2,6},{6,10},{10,14},{3,7},{... | collective-permute-start | bytes 786440 | tf_op jit(solution)/shard_map/ppermute | solution.py:25
  105.8 1.3 collective-permute-start.2
  107.1 3.8 %collective-permute-done.1 = bf16[4,1,64,512]{3,2,1,0:T(8,128)(2,1)S(1)} collective-permute-done((bf16[4,1,64,512]{3,2,1,0:T(8,128)(2,1)S(1)}, bf16[4,1,64,512]{3,2,1,0:T(8,128)(2,1)S(1)}, u32[]{:S(2)}, u32[]{:S(2)}) %collective-permute-start.1) | collective-permute-done | bytes 262176 | tf_op jit(solution)/shard_map/ppermute | solution.py:25
  110.9 4.1 %collective-permute-done.2 = bf16[4,1,64,512]{3,2,1,0:T(8,128)(2,1)S(1)} collective-permute-done((bf16[4,1,64,512]{3,2,1,0:T(8,128)(2,1)S(1)}, bf16[4,1,64,512]{3,2,1,0:T(8,128)(2,1)S(1)}, u32[]{:S(2)}, u32[]{:S(2)}) %collective-permute-start.2) | collective-permute-done | bytes 262176 | tf_op jit(solution)/shard_map/ppermute | solution.py:27
  115.0 0.2 fusion.13
  115.3 0.7 fusion.36
  116.0 0.8 fusion.35
  116.8 0.4 fusion.34
  117.2 1.3 fusion.20
  118.5 1.7 %fusion.19 = f32[128,256]{1,0:T(8,128)S(1)} fusion(bf16[128,512]{1,0:T(8,128)(2,1)S(1)} %bitcast.184, bf16[3,3,3,512,256]{4,3,2,1,0:T(8,128)(2,1)} %all-gather.2.cloned.1.call-done), kind=kOutput, calls=%fused_computation.69 | convolution fusion | flops 33554432 | bytes 524288 | tf_op jit(solution)/shard_map/dot_general | solution.py:102
  120.2 1.1 fusion.18
  121.4 1.1 fusion.17
  122.5 1.1 fusion.16
  123.7 1.2 fusion.15
  124.8 1.1 fusion.14
  126.0 1.1 convolution_add_fusion.19
  127.1 1.1 convolution_add_fusion.18
  128.3 1.1 convolution_add_fusion.17
  129.4 1.1 fusion.6
  130.6 1.1 convolution_add_fusion.15
  131.7 1.1 fusion.5
  132.8 0.2 convolution_add_fusion.13
  133.0 0.2 fusion.4
  133.2 0.2 convolution_add_fusion.11
  133.4 0.2 convolution_add_fusion.10
  133.6 0.2 convolution_add_fusion.9
  133.8 0.2 convolution_add_fusion.8
  134.0 0.2 fusion.3
  134.2 0.2 convolution_add_fusion.6
  134.4 0.2 fusion.2
  134.6 0.2 convolution_add_fusion.4
  134.8 0.2 convolution_add_fusion.3
  135.0 0.2 convolution_add_fusion.2
  135.2 0.2 convolution_add_fusion.1
  135.4 0.8 fusion.8
  136.3 0.6 copy.24
  (33 shorter events, 0.6 us)
Async XLA Ops:
  7.2 30.4 %copy-start = (bf16[512,512]{1,0:T(8,128)(2,1)S(1)}, bf16[512,512]{1,0:T(8,128)(2,1)}, u32[]{:S(2)}) copy-start(bf16[512,512]{1,0:T(8,128)(2,1)} %param.12) | copy-start | bytes 1572868
  7.2 67.0 %copy-start.2 = (bf16[2,1,64,256]{3,2,1,0:T(8,128)(2,1)S(1)}, bf16[2,1,64,256]{3,2,1,0:T(8,128)(2,1)}, u32[]{:S(2)}) copy-start(bf16[2,1,64,256]{3,2,1,0:T(8,128)(2,1)} %param.8) | copy-start | bytes 196612
  7.2 85.1 %copy-start.7 = (f32[256]{0:T(256)S(1)}, f32[256]{0:T(256)}, u32[]{:S(2)}) copy-start(f32[256]{0:T(256)} %param.10) | copy-start | bytes 3076
  7.2 110.0 %all-gather.2.cloned.1.call-start = ((), (), s32[]{:S(2)}) async-start(), calls=%async_computation.2 | async-start | bytes 10616832 | tf_op jit(solution)/shard_map/all_gather | solution.py:92
  94.3 8.4 %collective-permute-start = (bf16[2,1,64,512]{3,2,1,0:T(8,128)(2,1)S(1)}, bf16[2,1,64,512]{3,2,1,0:T(8,128)(2,1)S(1)}, u32[]{:S(2)}, u32[]{:S(2)}) collective-permute-start(bf16[2,1,64,512]{3,2,1,0:T(8,128)(2,1)S(1)} %all_gather.14), channel_id=1, source_target_pairs={{0,2},{1,3},{4,6},{5,7},{8,10},{9,11},{12,14},{13,15},{16,18},{17,... | collective-permute-start | bytes 393224 | tf_op jit(solution)/shard_map/ppermute | solution.py:14
  102.8 8.1 %collective-permute-start.1 = (bf16[4,1,64,512]{3,2,1,0:T(8,128)(2,1)S(1)}, bf16[4,1,64,512]{3,2,1,0:T(8,128)(2,1)S(1)}, u32[]{:S(2)}, u32[]{:S(2)}) collective-permute-start(bf16[4,1,64,512]{3,2,1,0:T(8,128)(2,1)S(1)} %constant_dynamic-update-slice_fusion), channel_id=1, source_target_pairs={{0,4},{4,8},{8,12},{1,5},{5,9},{9,13},{2,6},{6,10},{10,14},{3,7},{... | collective-permute-start | bytes 786440 | tf_op jit(solution)/shard_map/ppermute | solution.py:25
  105.8 9.2 %collective-permute-start.2 = (bf16[4,1,64,512]{3,2,1,0:T(8,128)(2,1)S(1)}, bf16[4,1,64,512]{3,2,1,0:T(8,128)(2,1)S(1)}, u32[]{:S(2)}, u32[]{:S(2)}) collective-permute-start(bf16[4,1,64,512]{3,2,1,0:T(8,128)(2,1)S(1)} %constant_dynamic-update-slice_fusion), channel_id=1, source_target_pairs={{4,0},{8,4},{12,8},{5,1},{9,5},{13,9},{6,2},{10,6},{14,10},{7,3},{... | collective-permute-start | bytes 786440 | tf_op jit(solution)/shard_map/ppermute | solution.py:27
  117.2 14.5 %copy-start.1 = (bf16[3,3,3,512,256]{4,3,2,1,0:T(8,128)(2,1)S(1)}, bf16[3,3,3,512,256]{4,3,2,1,0:T(8,128)(2,1)}, u32[]{:S(2)}) copy-start(bf16[3,3,3,512,256]{4,3,2,1,0:T(8,128)(2,1)} %all-gather.2.cloned.1.call-done) | copy-start | bytes 21233668
  117.2 15.8 %copy-start.6 = (bf16[2,1,64,512]{3,2,1,0:T(8,128)(2,1)S(1)}, bf16[2,1,64,512]{3,2,1,0:T(8,128)(2,1)}, u32[]{:S(2)}) copy-start(bf16[2,1,64,512]{3,2,1,0:T(8,128)(2,1)} %get-tuple-element.38) | copy-start | bytes 393220
  117.2 16.8 %copy-start.5 = (bf16[2,1,64,512]{3,2,1,0:T(8,128)(2,1)S(1)}, bf16[2,1,64,512]{3,2,1,0:T(8,128)(2,1)}, u32[]{:S(2)}) copy-start(bf16[2,1,64,512]{3,2,1,0:T(8,128)(2,1)} %get-tuple-element.35) | copy-start | bytes 393220
  117.2 17.2 %copy-start.4 = (bf16[2,1,64,512]{3,2,1,0:T(8,128)(2,1)S(1)}, bf16[2,1,64,512]{3,2,1,0:T(8,128)(2,1)}, u32[]{:S(2)}) copy-start(bf16[2,1,64,512]{3,2,1,0:T(8,128)(2,1)} %get-tuple-element.37) | copy-start | bytes 393220
  123.6 11.8 %copy-start.3 = (bf16[2,1,64,512]{3,2,1,0:T(8,128)(2,1)S(1)}, bf16[2,1,64,512]{3,2,1,0:T(8,128)(2,1)}, u32[]{:S(2)}) copy-start(bf16[2,1,64,512]{3,2,1,0:T(8,128)(2,1)} %get-tuple-element.34) | copy-start | bytes 393220
Sparse Core Ops, SparseCore 0:
  9.6 92.6 all-gather.1
where the time goes:
time: 145 us; the launch traced here: 144 us
  blocking collectives  78.5 us (54%)
  matrix products  23.1 us (16%)
  between operations  14.5 us (10%)
  waiting for transfers between devices  12.9 us (9%)
  starting transfers between devices  8.43 us (6%)
  local copies, waits for them, and re-layouts  3.52 us (2%)
  other arithmetic  2.8 us (2%)
    psum x2, blocking collectives, normalize(): lax.psum((jnp.sum(grouped, axis=(0, 2)), jnp.sum(grouped * grouped, axis=...  40.8 us
    dot_general x27, matrix products, convolve(): jnp.dot(window, piece[time_tap, row_tap, col_tap], preferred_element_type...  18.8 us
    all_gather x1, blocking collectives, attend(): key_piece = lax.all_gather(keyed, 'space', axis=0, tiled=True)  14.3 us
    all_gather x1, blocking collectives, attend(): value_piece = lax.all_gather(valued, 'space', axis=0, tiled=True)  13.9 us
    ppermute x1, waiting for transfers between devices, shifted_2(): return lax.ppermute(x, axis, pairs)  4.29 us
    ppermute x1, waiting for transfers between devices, padded_2(): lax.ppermute(head, axis, [((i + 1) % count, i) for i in range(ends)])  4.13 us
    ppermute x1, starting transfers between devices, shifted_2(): return lax.ppermute(x, axis, pairs)  4.12 us
    ppermute x1, waiting for transfers between devices, padded_2(): lax.ppermute(tail, axis, [(i, (i + 1) % count) for i in range(ends)])  3.8 us
  transfers between devices with their start and end apart: 4, of which 3 were waited for; matrix products, arithmetic and copies ran while one was open for 7% of the time, Pallas kernels for 0%

commit v1 on v0

--- a/solution.py
+++ b/solution.py
@@ -58,7 +58,14 @@
     score_scale = D ** (-0.5)
     running_max = jnp.full((half_rows,), -1e30, jnp.float32)
     key_piece = lax.all_gather(keyed, "space", axis=0, tiled=True)
-    value_piece = lax.all_gather(valued, "space", axis=0, tiled=True)
+    ring = [valued]
+    for hop in range(3):
+        ring.append(lax.ppermute(ring[-1], "space", [(dev, (dev + 1) % 4) for dev in range(4)]))
+    value_piece = jnp.roll(
+        jnp.concatenate(ring[::-1], axis=0),
+        (lax.axis_index("space") + 1) * ring[0].shape[0],
+        axis=0,
+    )
     scores = jnp.dot(queries, key_piece.T, preferred_element_type=jnp.float32) * score_scale
     newest_max = jnp.maximum(running_max, jnp.max(scores, axis=1))
     weights = jnp.exp(scores - newest_max[:, None])

time: 145 us -> 143 us (0.986)
  blocking collectives: 78.5 us -> 64.5 us
  waiting for transfers between devices: 12.9 us -> 24.8 us
    all_gather x1 -> x0, blocking collectives: 13.9 us -> none  [attend(): value_piece = lax.all_gather(valued, 'space', axis=0, tiled=True)]
    ppermute x0 -> x3, waiting for transfers between devices: none -> 9.48 us  [attend(): lax.ppermute(ring[-1], 'space', [(dev, (dev + 1) % 4) for dev in range(4)])]
    ppermute x0 -> x3, starting transfers between devices: none -> 2.95 us  [attend(): lax.ppermute(ring[-1], 'space', [(dev, (dev + 1) % 4) for dev in range(4)])]
    ppermute x1, waiting for transfers between devices: 4.29 us -> 6.44 us  [shifted_2(): return lax.ppermute(x, axis, pairs)]
    ppermute x1, starting transfers between devices: 2.98 us -> 1.31 us  [padded_2(): lax.ppermute(tail, axis, [(i, (i + 1) % count) for i in range(ends)])]
  transfers between devices with their start and end apart: 4 -> 7, of which waited for: 3 -> 5; matrix products, arithmetic and copies ran while one was open for 7% -> 6% of each run, Pallas kernels for 0% -> 0%
where the time goes in v1:
time: 143 us; the launch traced here: 142 us
  blocking collectives  64.5 us (45%)
  waiting for transfers between devices  24.8 us (17%)
  matrix products  22.1 us (15%)
  between operations  14.6 us (10%)
  starting transfers between devices  9.71 us (7%)
  local copies, waits for them, and re-layouts  3.57 us (2%)
  other arithmetic  2.79 us (2%)
    psum x2, blocking collectives, normalize(): lax.psum((jnp.sum(grouped, axis=(0, 2)), jnp.sum(grouped * grouped, axis=...  40.8 us
    dot_general x27, matrix products, convolve(): jnp.dot(window, piece[time_tap, row_tap, col_tap], preferred_element_type...  18.8 us
    all_gather x1, blocking collectives, attend(): key_piece = lax.all_gather(keyed, 'space', axis=0, tiled=True)  14.3 us
    ppermute x3, waiting for transfers between devices, attend(): lax.ppermute(ring[-1], 'space', [(dev, (dev + 1) % 4) for dev in range(4)])  9.48 us
    ppermute x1, waiting for transfers between devices, shifted_2(): return lax.ppermute(x, axis, pairs)  6.44 us
    ppermute x1, waiting for transfers between devices, padded_2(): lax.ppermute(head, axis, [((i + 1) % count, i) for i in range(ends)])  4.13 us
    ppermute x1, starting transfers between devices, shifted_2(): return lax.ppermute(x, axis, pairs)  4.12 us
    ppermute x1, waiting for transfers between devices, padded_2(): lax.ppermute(tail, axis, [(i, (i + 1) % count) for i in range(ends)])  4.08 us
  transfers between devices with their start and end apart: 7, of which 5 were waited for; matrix products, arithmetic and copies ran while one was open for 6% of the time, Pallas kernels for 0%

profile of v1, /device:TPU:0, one launch (start us, length us, event | category | flops | bytes accessed | tf_op | source)
XLA Modules:
  0.0 142.0 jit_solution(14323070120578416785)
XLA Ops:
  7.3 0.7 all-gather.2.cloned.1.call-update
  7.9 0.9 convert_reduce_fusion
  9.0 0.1 reduce_sum.59
  9.1 0.1 reduce_sum.62
  9.2 23.3 %all-reduce.2 = (f32[16]{0:T(128)S(1)}, f32[16]{0:T(128)S(1)}) all-reduce(f32[16]{0:T(128)S(1)} %reduce_sum.62, f32[16]{0:T(128)S(1)} %reduce_sum.59), channel_id=1, replica_groups=mesh['groups'=2,'space'=4,'tm'=2,'chan'=2] {'space','tm'}, use_global_device_ids=true, to_apply=%region_5.6 | all-reduce | flops 32 | bytes 256 | tf_op jit(solution)/shard_map/psum | solution.py:39
  32.6 0.1 mul.80
  32.8 0.1 sub.47
  32.9 0.9 fusion.28
  33.7 3.8 %all_to_all.35 = bf16[2,64,256]{2,1,0:T(8,128)(2,1)S(1)} all-to-all(bf16[2,64,256]{2,1,0:T(8,128)(2,1)S(1)} %fusion.28), channel_id=1, replica_groups=mesh['groups'=2,'space'=4,'tm'=2,'chan'=2] {'chan'}, dimensions={0} | all-to-all | bytes 131072 | tf_op jit(solution)/shard_map/all_to_all | solution.py:53
  37.5 0.2 convolution_convert_fusion.1
  37.8 1.2 convolution_convert_fusion.2
  39.1 14.3 %all_gather.9 = bf16[256,512]{1,0:T(8,128)(2,1)S(1)} all-gather(bf16[64,512]{1,0:T(8,128)(2,1)S(1)} %convolution_convert_fusion.2), channel_id=1, replica_groups=mesh['groups'=2,'space'=4,'tm'=2,'chan'=2] {'space'}, dimensions={0}, use_global_device_ids=true | all-gather | bytes 327680 | tf_op jit(solution)/shard_map/all_gather | solution.py:60
  53.3 1.5 %fusion.41 = (f32[64]{0:T(128)S(1)}, f32[64,256]{1,0:T(8,128)S(1)}) fusion(bf16[256,512]{1,0:T(8,128)(2,1)S(1)} %all_gather.9, bf16[64,512]{1,0:T(8,128)(2,1)S(1)} %bitcast.163, bf16[512,512]{1,0:T(8,128)(2,1)} %param.11), kind=kOutput, calls=%fused_computation.114 | convolution fusion | flops 50397120 | bytes 917760 | tf_op jit(solution)/shard_map/dot_general | solution.py:69
  54.8 2.3 %collective-permute-start.1 = (bf16[64,512]{1,0:T(8,128)(2,1)S(1)}, bf16[64,512]{1,0:T(8,128)(2,1)S(1)}, u32[]{:S(2)}, u32[]{:S(2)}) collective-permute-start(bf16[64,512]{1,0:T(8,128)(2,1)S(1)} %collective-permute-done), channel_id=1, source_target_pairs={{0,4},{4,8},{8,12},{12,0},{1,5},{5,9},{9,13},{13,1},{2,6},{6,10},{... | collective-permute-start | bytes 196616 | tf_op jit(solution)/shard_map/ppermute | solution.py:63
  57.1 4.2 %collective-permute-done.1 = bf16[64,512]{1,0:T(8,128)(2,1)S(1)} collective-permute-done((bf16[64,512]{1,0:T(8,128)(2,1)S(1)}, bf16[64,512]{1,0:T(8,128)(2,1)S(1)}, u32[]{:S(2)}, u32[]{:S(2)}) %collective-permute-start.1) | collective-permute-done | bytes 65568 | tf_op jit(solution)/shard_map/ppermute | solution.py:63
  61.3 0.6 collective-permute-start.2
  62.0 0.2 fusion.30
  62.1 5.2 %collective-permute-done.2 = bf16[64,512]{1,0:T(8,128)(2,1)S(1)} collective-permute-done((bf16[64,512]{1,0:T(8,128)(2,1)S(1)}, bf16[64,512]{1,0:T(8,128)(2,1)S(1)}, u32[]{:S(2)}, u32[]{:S(2)}) %collective-permute-start.2) | collective-permute-done | bytes 65568 | tf_op jit(solution)/shard_map/ppermute | solution.py:63
  67.5 0.4 convolution_convert_fusion
  67.9 3.8 %all_to_all.36 = bf16[64,2,256]{2,0,1:T(8,128)(2,1)S(1)} all-to-all(bf16[64,2,256]{2,0,1:T(8,128)(2,1)S(1)} %bitcast.192), channel_id=1, replica_groups=mesh['groups'=2,'space'=4,'tm'=2,'chan'=2] {'chan'}, dimensions={1} | all-to-all | bytes 131072 | tf_op jit(solution)/shard_map/all_to_all | solution.py:78
  71.8 0.1 reduce_sum.82
  72.0 0.1 reduce_sum.85
  72.1 17.4 %all-reduce.1 = (f32[16]{0:T(128)S(1)}, f32[16]{0:T(128)S(1)}) all-reduce(f32[16]{0:T(128)S(1)} %reduce_sum.85, f32[16]{0:T(128)S(1)} %reduce_sum.82), channel_id=1, replica_groups=mesh['groups'=2,'space'=4,'tm'=2,'chan'=2] {'space','tm'}, use_global_device_ids=true, to_apply=%region_13.14 | all-reduce | flops 32 | bytes 256 | tf_op jit(solution)/shard_map/psum | solution.py:39
  89.7 0.1 mul.91
  89.8 0.1 sub.55
  90.0 1.9 %all_gather.10 = bf16[2,1,64,512]{3,2,1,0:T(8,128)(2,1)S(1)} all-gather(bf16[2,1,64,256]{3,2,1,0:T(8,128)(2,1)S(1)} %multiply_convert_fusion), channel_id=1, replica_groups=mesh['groups'=2,'space'=4,'tm'=2,'chan'=2] {'chan'}, dimensions={3}, use_global_device_ids=true | all-gather | bytes 196608 | tf_op jit(solution)/shard_map/all_gather | solution.py:83
  91.9 4.1 %collective-permute-start.3 = (bf16[2,1,64,512]{3,2,1,0:T(8,128)(2,1)S(1)}, bf16[2,1,64,512]{3,2,1,0:T(8,128)(2,1)S(1)}, u32[]{:S(2)}, u32[]{:S(2)}) collective-permute-start(bf16[2,1,64,512]{3,2,1,0:T(8,128)(2,1)S(1)} %all_gather.10), channel_id=1, source_target_pairs={{0,2},{1,3},{4,6},{5,7},{8,10},{9,11},{12,14},{13,15},{16,18},{17,... | collective-permute-start | bytes 393224 | tf_op jit(solution)/shard_map/ppermute | solution.py:14
  96.0 6.4 %collective-permute-done.3 = bf16[2,1,64,512]{3,2,1,0:T(8,128)(2,1)S(1)} collective-permute-done((bf16[2,1,64,512]{3,2,1,0:T(8,128)(2,1)S(1)}, bf16[2,1,64,512]{3,2,1,0:T(8,128)(2,1)S(1)}, u32[]{:S(2)}, u32[]{:S(2)}) %collective-permute-start.3) | collective-permute-done | bytes 131104 | tf_op jit(solution)/shard_map/ppermute | solution.py:14
  102.5 1.3 collective-permute-start.4
  103.8 1.3 collective-permute-start.5
  105.1 4.1 %collective-permute-done.4 = bf16[4,1,64,512]{3,2,1,0:T(8,128)(2,1)S(1)} collective-permute-done((bf16[4,1,64,512]{3,2,1,0:T(8,128)(2,1)S(1)}, bf16[4,1,64,512]{3,2,1,0:T(8,128)(2,1)S(1)}, u32[]{:S(2)}, u32[]{:S(2)}) %collective-permute-start.4) | collective-permute-done | bytes 262176 | tf_op jit(solution)/shard_map/ppermute | solution.py:25
  109.2 4.1 %collective-permute-done.5 = bf16[4,1,64,512]{3,2,1,0:T(8,128)(2,1)S(1)} collective-permute-done((bf16[4,1,64,512]{3,2,1,0:T(8,128)(2,1)S(1)}, bf16[4,1,64,512]{3,2,1,0:T(8,128)(2,1)S(1)}, u32[]{:S(2)}, u32[]{:S(2)}) %collective-permute-start.5) | collective-permute-done | bytes 262176 | tf_op jit(solution)/shard_map/ppermute | solution.py:27
  113.3 0.2 fusion.13
  113.6 0.7 fusion.40
  114.3 0.8 fusion.39
  115.1 0.4 fusion.38
  115.5 1.3 fusion.20
  116.8 1.7 %fusion.19 = f32[128,256]{1,0:T(8,128)S(1)} fusion(bf16[128,512]{1,0:T(8,128)(2,1)S(1)} %bitcast.183, bf16[3,3,3,512,256]{4,3,2,1,0:T(8,128)(2,1)} %all-gather.2.cloned.1.call-done), kind=kOutput, calls=%fused_computation.69 | convolution fusion | flops 33554432 | bytes 524288 | tf_op jit(solution)/shard_map/dot_general | solution.py:109
  118.5 1.1 fusion.18
  119.7 1.1 fusion.17
  120.8 1.1 fusion.16
  122.0 1.2 fusion.15
  123.1 1.1 fusion.14
  124.3 1.1 convolution_add_fusion.19
  125.4 1.1 convolution_add_fusion.18
  126.6 1.1 convolution_add_fusion.17
  127.7 1.1 fusion.6
  128.9 1.1 convolution_add_fusion.15
  130.0 1.1 fusion.5
  131.1 0.2 convolution_add_fusion.13
  131.3 0.2 fusion.4
  131.5 0.2 convolution_add_fusion.11
  131.7 0.2 convolution_add_fusion.10
  131.9 0.2 convolution_add_fusion.9
  132.1 0.2 convolution_add_fusion.8
  132.3 0.2 fusion.3
  132.5 0.2 convolution_add_fusion.6
  132.7 0.2 fusion.2
  132.9 0.2 convolution_add_fusion.4
  133.1 0.2 convolution_add_fusion.3
  133.3 0.2 convolution_add_fusion.2
  133.5 0.2 convolution_add_fusion.1
  133.7 0.8 fusion.8
  134.6 0.6 copy.31
  (48 shorter events, 1.0 us)
Async XLA Ops:
  7.2 30.4 %copy-start = (bf16[512,512]{1,0:T(8,128)(2,1)S(1)}, bf16[512,512]{1,0:T(8,128)(2,1)}, u32[]{:S(2)}) copy-start(bf16[512,512]{1,0:T(8,128)(2,1)} %param.13) | copy-start | bytes 1572868
  7.2 64.5 %copy-start.2 = (bf16[2,1,64,256]{3,2,1,0:T(8,128)(2,1)S(1)}, bf16[2,1,64,256]{3,2,1,0:T(8,128)(2,1)}, u32[]{:S(2)}) copy-start(bf16[2,1,64,256]{3,2,1,0:T(8,128)(2,1)} %param.8) | copy-start | bytes 196612
  7.2 60.3 %copy-start.8 = (bf16[512,512]{1,0:T(8,128)(2,1)S(1)}, bf16[512,512]{1,0:T(8,128)(2,1)}, u32[]{:S(2)}) copy-start(bf16[512,512]{1,0:T(8,128)(2,1)} %param.14) | copy-start | bytes 1572868
  7.2 82.7 %copy-start.7 = (f32[256]{0:T(256)S(1)}, f32[256]{0:T(256)}, u32[]{:S(2)}) copy-start(f32[256]{0:T(256)} %param.10) | copy-start | bytes 3076
  7.2 108.3 %all-gather.2.cloned.1.call-start = ((), (), s32[]{:S(2)}) async-start(), calls=%async_computation.2 | async-start | bytes 10616832 | tf_op jit(solution)/shard_map/all_gather | solution.py:99
  37.8 17.1 %collective-permute-start = (bf16[64,512]{1,0:T(8,128)(2,1)S(1)}, bf16[64,512]{1,0:T(8,128)(2,1)S(1)}, u32[]{:S(2)}, u32[]{:S(2)}) collective-permute-start(bf16[64,512]{1,0:T(8,128)(2,1)S(1)} %convolution_convert_fusion.1), channel_id=1, source_target_pairs={{0,4},{4,8},{8,12},{12,0},{1,5},{5,9},{9,13},{13,1},{2,6},{6,10},{... | collective-permute-start | bytes 196616 | tf_op jit(solution)/shard_map/ppermute | solution.py:63
  54.8 6.5 %collective-permute-start.1 = (bf16[64,512]{1,0:T(8,128)(2,1)S(1)}, bf16[64,512]{1,0:T(8,128)(2,1)S(1)}, u32[]{:S(2)}, u32[]{:S(2)}) collective-permute-start(bf16[64,512]{1,0:T(8,128)(2,1)S(1)} %collective-permute-done), channel_id=1, source_target_pairs={{0,4},{4,8},{8,12},{12,0},{1,5},{5,9},{9,13},{13,1},{2,6},{6,10},{... | collective-permute-start | bytes 196616 | tf_op jit(solution)/shard_map/ppermute | solution.py:63
  61.3 6.1 %collective-permute-start.2 = (bf16[64,512]{1,0:T(8,128)(2,1)S(1)}, bf16[64,512]{1,0:T(8,128)(2,1)S(1)}, u32[]{:S(2)}, u32[]{:S(2)}) collective-permute-start(bf16[64,512]{1,0:T(8,128)(2,1)S(1)} %collective-permute-done.1), channel_id=1, source_target_pairs={{0,4},{4,8},{8,12},{12,0},{1,5},{5,9},{9,13},{13,1},{2,6},{6,10},{... | collective-permute-start | bytes 196616 | tf_op jit(solution)/shard_map/ppermute | solution.py:63
  91.9 10.6 %collective-permute-start.3 = (bf16[2,1,64,512]{3,2,1,0:T(8,128)(2,1)S(1)}, bf16[2,1,64,512]{3,2,1,0:T(8,128)(2,1)S(1)}, u32[]{:S(2)}, u32[]{:S(2)}) collective-permute-start(bf16[2,1,64,512]{3,2,1,0:T(8,128)(2,1)S(1)} %all_gather.10), channel_id=1, source_target_pairs={{0,2},{1,3},{4,6},{5,7},{8,10},{9,11},{12,14},{13,15},{16,18},{17,... | collective-permute-start | bytes 393224 | tf_op jit(solution)/shard_map/ppermute | solution.py:14
  102.5 6.7 %collective-permute-start.4 = (bf16[4,1,64,512]{3,2,1,0:T(8,128)(2,1)S(1)}, bf16[4,1,64,512]{3,2,1,0:T(8,128)(2,1)S(1)}, u32[]{:S(2)}, u32[]{:S(2)}) collective-permute-start(bf16[4,1,64,512]{3,2,1,0:T(8,128)(2,1)S(1)} %constant_dynamic-update-slice_fusion.8), channel_id=1, source_target_pairs={{0,4},{4,8},{8,12},{1,5},{5,9},{9,13},{2,6},{6,10},{10,14},{3,7},{... | collective-permute-start | bytes 786440 | tf_op jit(solution)/shard_map/ppermute | solution.py:25
  103.8 9.5 %collective-permute-start.5 = (bf16[4,1,64,512]{3,2,1,0:T(8,128)(2,1)S(1)}, bf16[4,1,64,512]{3,2,1,0:T(8,128)(2,1)S(1)}, u32[]{:S(2)}, u32[]{:S(2)}) collective-permute-start(bf16[4,1,64,512]{3,2,1,0:T(8,128)(2,1)S(1)} %constant_dynamic-update-slice_fusion.8), channel_id=1, source_target_pairs={{4,0},{8,4},{12,8},{5,1},{9,5},{13,9},{6,2},{10,6},{14,10},{7,3},{... | collective-permute-start | bytes 786440 | tf_op jit(solution)/shard_map/ppermute | solution.py:27
  115.5 14.5 %copy-start.1 = (bf16[3,3,3,512,256]{4,3,2,1,0:T(8,128)(2,1)S(1)}, bf16[3,3,3,512,256]{4,3,2,1,0:T(8,128)(2,1)}, u32[]{:S(2)}) copy-start(bf16[3,3,3,512,256]{4,3,2,1,0:T(8,128)(2,1)} %all-gather.2.cloned.1.call-done) | copy-start | bytes 21233668
  115.5 15.8 %copy-start.6 = (bf16[2,1,64,512]{3,2,1,0:T(8,128)(2,1)S(1)}, bf16[2,1,64,512]{3,2,1,0:T(8,128)(2,1)}, u32[]{:S(2)}) copy-start(bf16[2,1,64,512]{3,2,1,0:T(8,128)(2,1)} %get-tuple-element.38) | copy-start | bytes 393220
  115.5 16.8 %copy-start.5 = (bf16[2,1,64,512]{3,2,1,0:T(8,128)(2,1)S(1)}, bf16[2,1,64,512]{3,2,1,0:T(8,128)(2,1)}, u32[]{:S(2)}) copy-start(bf16[2,1,64,512]{3,2,1,0:T(8,128)(2,1)} %get-tuple-element.35) | copy-start | bytes 393220
  115.5 17.2 %copy-start.4 = (bf16[2,1,64,512]{3,2,1,0:T(8,128)(2,1)S(1)}, bf16[2,1,64,512]{3,2,1,0:T(8,128)(2,1)}, u32[]{:S(2)}) copy-start(bf16[2,1,64,512]{3,2,1,0:T(8,128)(2,1)} %get-tuple-element.37) | copy-start | bytes 393220
  121.9 11.8 %copy-start.3 = (bf16[2,1,64,512]{3,2,1,0:T(8,128)(2,1)S(1)}, bf16[2,1,64,512]{3,2,1,0:T(8,128)(2,1)}, u32[]{:S(2)}) copy-start(bf16[2,1,64,512]{3,2,1,0:T(8,128)(2,1)} %get-tuple-element.34) | copy-start | bytes 393220
Sparse Core Ops, SparseCore 0:
  9.6 93.2 all-gather.1
